TPU v7x, 32 devices: a whole 2x2x4 slice. The times are simulated.
32 devices in a mesh: pair: 4 (over y, core), fold: 8 (over z, x).
Axes of the slice: x: 2, y: 2, z: 4, core: 2. Of those that a mesh axis runs over, the one named last changes fastest.
Arguments:
- amplitudes: bfloat16 [4, 80, 640, 640], P(None, 'pair', 'fold'), may hold values from -6 to 6
- cycle_block: bfloat16 [640, 80, 8, 640], P('fold', None, 'pair'), may hold values from -0.078125 to 0.078125
- occ_sizes: int32 [8], replicated, may hold values from 1 to 20, 80 in all
- vir_sizes: int32 [8], replicated, may hold values from 1 to 160, 640 in all
- window_i: int32 [4], replicated, may hold values from 0 to 79
- window_occ: int32 [8], replicated, may hold values from 0 to 79
Outputs:
- residual: bfloat16 [4, 640, 8, 640], P(None, 'fold', 'pair')
Inputs may be any that keep to these rules, and one draw needn't show every extreme that they name: `occ_sizes`: the entries sum to 80. `vir_sizes`: the entries sum to 640.
All inputs are finite; a program needn't handle non-finite values.
Results may differ from a plain program's by a relative error of at most 0.001.
Values may be sent and summed in bfloat16 or wider, within the bound.
A program may use at most 128 MiB of HBM per device.

v0:
```python
import jax
import jax.numpy as jnp
from jax import lax
from jax.sharding import PartitionSpec as P


def irrep_labels(sizes, count):
    boundaries = jnp.cumsum(sizes)
    positions = jnp.arange(count, dtype=jnp.int32)
    return jnp.sum((positions[:, None] >= boundaries[None, :]).astype(jnp.int32), axis=1)


def label_lookup(orbitals, labels, count):
    matches = orbitals[:, None] == jnp.arange(count, dtype=jnp.int32)[None, :]
    return jnp.sum(jnp.where(matches, labels[None, :], 0), axis=1)


def body(amplitudes, cycle_block, occ_sizes, vir_sizes, window_i, window_occ):
    c_local = cycle_block.shape[0]
    occ_total = cycle_block.shape[1]
    j_local = cycle_block.shape[2]
    vir_total = cycle_block.shape[3]
    k_local = amplitudes.shape[1]
    a_rows = amplitudes.shape[2]
    occ_labels = irrep_labels(occ_sizes, occ_total)
    vir_labels = irrep_labels(vir_sizes, vir_total)
    c_labels = lax.dynamic_slice_in_dim(vir_labels, lax.axis_index("fold") * c_local, c_local)
    a_labels = lax.dynamic_slice_in_dim(vir_labels, lax.axis_index("fold") * a_rows, a_rows)
    k_labels = lax.dynamic_slice_in_dim(occ_labels, lax.axis_index("pair") * k_local, k_local)
    i_labels = label_lookup(window_i, occ_labels, occ_total)
    j_orbitals = lax.dynamic_slice_in_dim(window_occ, lax.axis_index("pair") * j_local, j_local)
    j_labels = label_lookup(j_orbitals, occ_labels, occ_total)
    amp_parity = jnp.bitwise_xor(
        jnp.bitwise_xor(i_labels[:, None, None, None], k_labels[None, :, None, None]),
        jnp.bitwise_xor(a_labels[None, None, :, None], vir_labels[None, None, None, :]),
    )
    masked_amps = jnp.where(amp_parity == 0, amplitudes, jnp.zeros_like(amplitudes))
    parity = jnp.bitwise_xor(
        jnp.bitwise_xor(c_labels[:, None, None, None], occ_labels[None, :, None, None]),
        jnp.bitwise_xor(j_labels[None, None, :, None], vir_labels[None, None, None, :]),
    )
    masked = jnp.where(parity == 0, cycle_block, jnp.zeros_like(cycle_block))
    relaid = lax.all_to_all(masked_amps, "fold", split_axis=3, concat_axis=2, tiled=True)
    gathered = lax.all_gather(relaid, "pair", axis=1, tiled=True)
    partial_sum = jnp.einsum(
        "ikac,ckjb->iajb", gathered, masked, preferred_element_type=jnp.float32
    )
    own_share = lax.psum_scatter(partial_sum, "fold", scatter_dimension=1, tiled=True)
    return own_share.astype(jnp.bfloat16)


def solution(mesh):
    placed = (P(None, "pair", "fold", None), P("fold", None, "pair", None), P(), P(), P(), P())
    return jax.shard_map(
        body, mesh=mesh, in_specs=placed, out_specs=P(None, "fold", "pair", None), check_vma=False
    )
```

profile of v0, /device:TPU:0, one launch (start us, length us, event | category | flops | bytes accessed | tf_op | source)
XLA Modules:
  0.0 913.6 jit_solution(13160478728247524786)
XLA Ops:
  6.5 0.8 reduce-window.16
  7.4 0.1 convert_reduce_fusion.1
  7.5 0.1 dynamic_slice.10
  7.5 0.8 select_reduce_fusion
  8.4 0.8 reduce-window.17
  9.2 0.1 convert_reduce_fusion
  9.3 0.1 dynamic_slice.11
  9.4 0.1 broadcast_xor_fusion
  9.5 18.2 %copy.20 = bf16[4,20,80,640]{2,1,0,3:T(8,128)(2,1)} copy(bf16[4,20,80,640]{3,2,1,0:T(8,128)(2,1)} %param.6) | data formatting | bytes 16384000 | tf_op args[0]
  27.8 10.3 %fusion.2 = bf16[4,20,80,640]{2,1,0,3:T(8,128)(2,1)S(1)} fusion(bf16[4,20,80,640]{2,1,0,3:T(8,128)(2,1)} %copy.20, s32[80,640]{0,1:T(8,128)S(1)} %broadcast_xor_fusion, s32[4,20]{1,0:T(4,128)S(1)} %broadcast_xor_fusion.3), kind=kLoop, calls=%fused_computation.4 | loop fusion | flops 12288000 | bytes 16589120 | tf_op jit(solution)/shard_map/jit(_where)/select_n | solution.py:37
  38.1 347.4 %all_to_all.18 = bf16[4,20,80,640]{2,1,0,3:T(8,128)(2,1)S(1)} all-to-all(bf16[4,20,80,640]{2,1,0,3:T(8,128)(2,1)S(1)} %fusion.2), channel_id=1, replica_groups=mesh['pair'=4,'fold'=8] {'fold'}, dimensions={3} | all-to-all | bytes 16384000 | tf_op jit(solution)/shard_map/all_to_all | solution.py:43
  385.5 9.7 %copy.44 = bf16[4,20,80,8,80]{2,3,4,1,0:T(8,128)(2,1)} copy(bf16[4,20,80,8,80]{2,1,0,4,3:T(8,128)(2,1)S(1)} %bitcast.28) | data formatting | bytes 16384000 | tf_op jit(solution)/shard_map/all_to_all | solution.py:43
  395.2 19.4 %all_to_all.16 = bf16[4,20,640,80]{2,3,1,0:T(8,128)(2,1)} reshape(bf16[4,20,8,80,80]{3,2,4,1,0:T(8,128)(2,1)} %bitcast.29) | data formatting | bytes 16384000 | tf_op jit(solution)/shard_map/all_to_all | solution.py:43
  414.6 7.7 copy.22
  422.5 0.1 dynamic_slice.12
  422.5 0.2 fusion.10
  422.7 0.1 broadcast_xor_fusion.2
  422.8 0.1 broadcast_xor_fusion.1
  422.9 26.6 %compare_select_fusion = bf16[80,80,2,640]{3,2,1,0:T(2,128)(2,1)} fusion(bf16[80,80,2,640]{3,2,1,0:T(2,128)(2,1)} %param.7, s32[2,640]{1,0:T(2,128)S(1)} %broadcast_xor_fusion.2, s32[80,80]{1,0:T(8,128)S(1)} %broadcast_xor_fusion.1), kind=kLoop, calls=%fused_computation | loop fusion | flops 24576000 | bytes 32798720 | tf_op jit(solution)/shard_map/jit(_where)/select_n | solution.py:42
  449.5 169.1 %all-gather.2.cloned.1.call-done = bf16[4,80,640,80]{2,3,0,1:T(8,128)(2,1)} async-done(((bf16[4,20,640,80]{2,3,0,1:T(8,128)(2,1)}), bf16[4,80,640,80]{2,3,0,1:T(8,128)(2,1)}) %all-gather.2.cloned.1.call-update) | async-done | bytes 32768016 | tf_op jit(solution)/shard_map/all_gather | solution.py:44
  618.6 70.1 %fusion.5 = f32[4,640,2,640]{3,1,2,0:T(8,128)} fusion(bf16[80,80,2,640]{3,2,1,0:T(2,128)(2,1)} %compare_select_fusion, bf16[4,80,640,80]{2,3,0,1:T(8,128)(2,1)} %all-gather.2.cloned.1.call-done), kind=kOutput, calls=%fused_computation.8 | convolution fusion | flops 41943040000 | bytes 62259200 | tf_op jit(solution)/shard_map/ikac,ckjb->iajb/dot_general | solution.py:45
  688.8 214.9 %reduce-scatter.2.cloned.1.call-done = f32[4,80,2,640]{3,1,2,0:T(8,128)} async-done(((f32[4,640,2,640]{3,1,2,0:T(8,128)}), f32[4,80,2,640]{3,1,2,0:T(8,128)}) %reduce-scatter.2.cloned.1.call-update) | async-done | bytes 1638416 | tf_op jit(solution)/shard_map/reduce_scatter | solution.py:48
  903.7 1.5 convert_element_type.11
  905.2 1.5 copy.25
  (7 shorter events, 0.2 us)
Async XLA Ops:
  6.5 612.1 %all-gather.2.cloned.1.call-start = ((), (), s32[]{:S(2)}) async-start(), calls=%async_computation.2 | async-start | bytes 40960000 | tf_op jit(solution)/shard_map/all_gather | solution.py:44
  414.6 7.8 copy-start
  422.4 481.3 %reduce-scatter.2.cloned.1.call-start = ((), (), s32[]{:S(2)}) async-start(), calls=%async_computation.3 | async-start | bytes 14745600 | tf_op jit(solution)/shard_map/reduce_scatter | solution.py:48
Sparse Core Ops, SparseCore 0:
  422.5 196.0 all-gather.1
  688.9 214.7 reduce-scatter.1
where the time goes:
time: 915 us; the launch traced here: 914 us
  waiting for transfers between devices  384 us (42%)
  blocking collectives  347 us (38%)
  matrix products  70.1 us (8%)
  local copies, waits for them, and re-layouts  56.8 us (6%)
  other arithmetic  41.7 us (5%)
  between operations  13.4 us (1%)
    all_to_all x1, blocking collectives, body(): lax.all_to_all(masked_amps, 'fold', split_axis=3, concat_axis=2, tiled=True)  347 us
    reduce_scatter x1, waiting for transfers between devices, body(): lax.psum_scatter(partial_sum, 'fold', scatter_dimension=1, tiled=True)  215 us
    all_gather x1, waiting for transfers between devices, body(): gathered = lax.all_gather(relaid, 'pair', axis=1, tiled=True)  169 us
    dot_general x1, matrix products, body(): jnp.einsum('ikac,ckjb->iajb', gathered, masked, preferred_element_type=jn...  70.1 us
    all_to_all x3, local copies, waits for them, and re-layouts, body(): lax.all_to_all(masked_amps, 'fold', split_axis=3, concat_axis=2, tiled=True)  36.8 us
    select_n x1, other arithmetic, body(): masked = jnp.where(parity == 0, cycle_block, jnp.zeros_like(cycle_block))  26.6 us
  transfers between devices with their start and end apart: 2, of which 2 were waited for; matrix products, arithmetic and copies ran while one was open for 3% of the time, Pallas kernels for 0%

commit v1 on v0

v1 whole, which is shorter than its diff:
```python
import jax
import jax.numpy as jnp
from jax import lax
from jax.sharding import PartitionSpec as P

FOLDS = 4


def irrep_labels(sizes, count):
    boundaries = jnp.cumsum(sizes)
    positions = jnp.arange(count, dtype=jnp.int32)
    return jnp.sum((positions[:, None] >= boundaries[None, :]).astype(jnp.int32), axis=1)


def label_lookup(orbitals, labels, count):
    matches = orbitals[:, None] == jnp.arange(count, dtype=jnp.int32)[None, :]
    return jnp.sum(jnp.where(matches, labels[None, :], 0), axis=1)


def body(n_pair, n_fold, amplitudes, cycle_block, occ_sizes, vir_sizes, window_i, window_occ):
    c_local, occ_total, j_local, vir_total = cycle_block.shape
    n_i, k_local, a_rows, _ = amplitudes.shape
    v_pack = vir_total // FOLDS
    k_pack = occ_total // FOLDS
    a_sub = a_rows // n_pair
    fold = lax.axis_index("fold")
    pair = lax.axis_index("pair")
    occ_labels = irrep_labels(occ_sizes, occ_total)
    vir_labels = irrep_labels(vir_sizes, vir_total)
    c_labels = lax.dynamic_slice_in_dim(vir_labels, fold * c_local, c_local)
    a_labels = lax.dynamic_slice_in_dim(vir_labels, fold * a_rows, a_rows)
    k_labels = lax.dynamic_slice_in_dim(occ_labels, pair * k_local, k_local)
    i_labels = label_lookup(window_i, occ_labels, occ_total)
    j_orbitals = lax.dynamic_slice_in_dim(window_occ, pair * j_local, j_local)
    j_labels = label_lookup(j_orbitals, occ_labels, occ_total)

    ika = i_labels[:, None, None] ^ k_labels[None, :, None] ^ a_labels[None, None, :]
    packed_c = 0
    for q in range(FOLDS):
        cut = slice(q * v_pack, (q + 1) * v_pack)
        keep = ika[..., None] == vir_labels[cut]
        packed_c = packed_c + jnp.where(keep, amplitudes[..., cut], 0)
    moved = lax.all_to_all(
        packed_c.reshape(n_i, k_local, n_pair, a_sub, v_pack), "pair", split_axis=2, concat_axis=1, tiled=True
    ).reshape(n_i, FOLDS, k_pack, a_sub, v_pack)
    own_a = lax.dynamic_slice_in_dim(a_labels, pair * a_sub, a_sub)
    ia = i_labels[:, None] ^ own_a[None, :]
    pieces = []
    for q in range(FOLDS):
        iac = ia[..., None] ^ vir_labels[q * v_pack:(q + 1) * v_pack]
        total = 0
        for s in range(FOLDS):
            keep = iac[:, None] == occ_labels[s * k_pack:(s + 1) * k_pack][None, :, None, None]
            total = total + jnp.where(keep, moved[:, s], 0)
        pieces.append(total)
    packed_k = jnp.concatenate(pieces, axis=-1)
    packed_k = packed_k.reshape(n_i, k_pack, a_sub, n_fold, c_local).transpose(3, 0, 2, 1, 4)
    packed_k = packed_k.reshape(n_fold, n_i * a_sub, k_pack * c_local)
    relaid = lax.all_to_all(packed_k, "fold", split_axis=0, concat_axis=0, tiled=True)
    gathered = lax.all_gather(relaid, "pair", axis=0, tiled=False)

    ckj = c_labels[:, None, None] ^ occ_labels[None, :, None] ^ j_labels[None, None, :]
    packed_w = 0
    for q in range(FOLDS):
        cut = slice(q * v_pack, (q + 1) * v_pack)
        keep = ckj[..., None] == vir_labels[cut]
        packed_w = packed_w + jnp.where(keep, cycle_block[..., cut], 0)
    packed_w = packed_w.reshape(c_local, FOLDS, k_pack, j_local * v_pack).transpose(1, 2, 0, 3)
    packed_w = packed_w.reshape(FOLDS, k_pack * c_local, j_local * v_pack)

    row_a = vir_labels.reshape(n_fold, n_pair, a_sub).transpose(1, 0, 2)
    row_labels = (row_a[:, :, None, :] ^ i_labels[:, None]).reshape(n_pair, n_fold, n_i * a_sub)
    partial_sum = 0
    for s in range(FOLDS):
        col_labels = (occ_labels[s * k_pack:(s + 1) * k_pack][:, None] ^ c_labels[None, :]).reshape(-1)
        lhs = jnp.where(row_labels[..., None] == col_labels, gathered, 0)
        partial_sum = partial_sum + jnp.einsum(
            "pfrx,xn->fprn", lhs, packed_w[s], preferred_element_type=jnp.float32
        )
    flat = partial_sum.reshape(-1, j_local * v_pack)
    own = lax.psum_scatter(flat, "fold", scatter_dimension=0, tiled=True)
    own = own.astype(jnp.bfloat16).reshape(n_pair, n_i, a_sub, j_local, v_pack)
    own = own.transpose(1, 0, 2, 3, 4).reshape(n_i, a_rows, j_local, v_pack)
    iaj = i_labels[:, None, None] ^ a_labels[None, :, None] ^ j_labels[None, None, :]
    keep = iaj[..., None] == vir_labels
    return jnp.where(keep, jnp.concatenate([own] * FOLDS, axis=-1), 0)


def solution(mesh):
    sizes = mesh.shape["pair"], mesh.shape["fold"]
    placed = (P(None, "pair", "fold", None), P("fold", None, "pair", None), P(), P(), P(), P())

    def run(*args):
        return body(*sizes, *args)

    return jax.shard_map(
        run, mesh=mesh, in_specs=placed, out_specs=P(None, "fold", "pair", None), check_vma=False
    )
```

time: 915 us -> 387 us (0.42)
  blocking collectives: 347 us -> 55.9 us
  waiting for transfers between devices: 384 us -> 117 us
  other arithmetic: 41.7 us -> 98.4 us
  matrix products: 70.1 us -> 30.7 us
    all_to_all x1, blocking collectives: 347 us -> 55.9 us  [body(): lax.all_to_all(packed_k, 'fold', split_axis=0, concat_axis=0, tiled=True)]
    all_gather x1, waiting for transfers between devices: 169 us -> 0.01 us  [body(): gathered = lax.all_gather(relaid, 'pair', axis=0, tiled=False)]
    reduce_scatter x1, waiting for transfers between devices: 215 us -> 82.2 us  [body(): own = lax.psum_scatter(flat, 'fold', scatter_dimension=0, tiled=True)]
    add x0 -> x3, other arithmetic: none -> 82.2 us  [the longest x1 56.1 us: body(): packed_w = packed_w + jnp.where(keep, cycle_block[..., cut], 0)]
    dot_general x1 -> x4, matrix products: 70.1 us -> 30.7 us  [body(): jnp.einsum('pfrx,xn->fprn', lhs, packed_w[s], preferred_element_type=jnp....]
    all_to_all x3 -> x0, local copies, waits for them, and re-layouts: 36.8 us -> none  [body(): lax.all_to_all(masked_amps, 'fold', split_axis=3, concat_axis=2, tiled=True)]
    all_to_all x0 -> x1, waiting for transfers between devices: none -> 34.4 us  [body(): lax.all_to_all(packed_c.reshape(n_i, k_local, n_pair, a_sub, v_pack), 'pa...]
    select_n x2 -> x1, other arithmetic: 37 us -> 4.45 us  [body(): return jnp.where(keep, jnp.concatenate([own] * FOLDS, axis=-1), 0)]
  transfers between devices with their start and end apart: 2 -> 3, of which waited for: 2 -> 2; matrix products, arithmetic and copies ran while one was open for 3% -> 23% of each run, Pallas kernels for 0% -> 0%
where the time goes in v1:
time: 387 us; the launch traced here: 380 us
  waiting for transfers between devices  117 us (30%)
  other arithmetic  98.4 us (25%)
  local copies, waits for them, and re-layouts  60.5 us (16%)
  blocking collectives  55.9 us (14%)
  matrix products  30.7 us (8%)
  between operations  13.9 us (4%)
  starting transfers between devices  4.31 us (1%)
    reduce_scatter x1, waiting for transfers between devices, body(): own = lax.psum_scatter(flat, 'fold', scatter_dimension=0, tiled=True)  82.2 us
    add x1, other arithmetic, body(): packed_w = packed_w + jnp.where(keep, cycle_block[..., cut], 0)  56.1 us
    all_to_all x1, blocking collectives, body(): lax.all_to_all(packed_k, 'fold', split_axis=0, concat_axis=0, tiled=True)  55.9 us
    all_to_all x1, waiting for transfers between devices, body(): lax.all_to_all(packed_c.reshape(n_i, k_local, n_pair, a_sub, v_pack), 'pa...  34.4 us
    dot_general x4, matrix products, body(): jnp.einsum('pfrx,xn->fprn', lhs, packed_w[s], preferred_element_type=jnp....  30.7 us
    reshape x2, local copies, waits for them, and re-layouts, body(): packed_w.reshape(c_local, FOLDS, k_pack, j_local * v_pack)  21.9 us
    add x1, other arithmetic, body(): total = total + jnp.where(keep, moved[:, s], 0)  16.6 us
    squeeze x4, local copies, waits for them, and re-layouts, body(): total = total + jnp.where(keep, moved[:, s], 0)  10.1 us
  transfers between devices with their start and end apart: 3, of which 2 were waited for; matrix products, arithmetic and copies ran while one was open for 23% of the time, Pallas kernels for 0%

profile of v1, /device:TPU:0, one launch (start us, length us, event | category | flops | bytes accessed | tf_op | source)
XLA Modules:
  0.0 380.3 jit_solution(2479154911337334194)
XLA Ops:
  10.2 9.5 %fusion.21 = bf16[4,20,80,160]{3,2,1,0:T(8,128)(2,1)S(1)} fusion(bf16[4,20,80,640]{3,2,1,0:T(8,128)(2,1)} %param.6, s32[160]{0:T(256)S(1)} %get-tuple-element.22, s32[160]{0:T(256)S(1)} %get-tuple-element.23, s32[160]{0:T(256)S(1)} %get-tuple-element.24, s32[160]{0:T(256)S(1)} %get-tuple-element.21, s32[4,20,80]{2,1,0:T(8,128)S(1)} %broadcast_xor_fusion.6), kind=kLoop, calls=%fused_computation.35 | loop fusion | flops 11264000 | bytes 10268160 | tf_op jit(solution)/shard_map/add | solution.py:42
  19.8 2.5 copy.45
  22.3 2.9 copy.46
  25.2 4.3 %all-to-all-start = ((bf16[4,20,4,20,160]{4,0,3,1,2:T(4,128)(2,1)}), bf16[4,20,4,20,160]{4,0,3,1,2:T(4,128)(2,1)S(1)}, u32[]{:S(2)}, u32[]{:S(2)}) async-start(bf16[4,20,4,20,160]{4,0,3,1,2:T(4,128)(2,1)} %copy.46), calls=%async_computation | async-start | bytes 6553600 | tf_op jit(solution)/shard_map/all_to_all | solution.py:43
  33.5 34.4 %all-to-all-done = bf16[4,20,4,20,160]{4,0,3,1,2:T(4,128)(2,1)S(1)} async-done(((bf16[4,20,4,20,160]{4,0,3,1,2:T(4,128)(2,1)}), bf16[4,20,4,20,160]{4,0,3,1,2:T(4,128)(2,1)S(1)}, u32[]{:S(2)}, u32[]{:S(2)}) %all-to-all-start) | async-done | bytes 2048032 | tf_op jit(solution)/shard_map/all_to_all | solution.py:43
  67.9 2.6 fusion.40
  70.5 2.7 squeeze.17
  73.1 2.5 squeeze.18
  75.6 2.5 squeeze.19
  80.7 16.6 %fusion.24 = (bf16[4,20,20,2,80]{4,3,0,2,1:T(2,128)(2,1)S(1)}, bf16[4,20,20,2,80]{4,3,0,2,1:T(2,128)(2,1)S(1)}, bf16[4,20,20,2,80]{4,3,0,2,1:T(2,128)(2,1)S(1)}, bf16[4,20,20,2,80]{4,3,0,2,1:T(2,128)(2,1)S(1)}) fusion(bf16[4,20,20,2,80]{4,3,0,2,1:T(2,128)(2,1)S(1)} %squeeze.40, s32[4,20,2,80]{3,2,0,1:T(2,128)S(1)} %get-tuple-element.17, ...), kind=kLoop, calls=%fused_computation.57 | loop fusion | flops 11264000 | bytes 4301120 | tf_op jit(solution)/shard_map/add | solution.py:54
  97.3 4.9 %maximum_bitcast_fusion = bf16[8,4,20,20,80]{4,0,1,2,3:T(8,128)(2,1)S(1)} fusion(bf16[4,20,20,2,80]{4,3,0,2,1:T(2,128)(2,1)S(1)} %get-tuple-element.10, bf16[4,20,20,2,80]{4,3,0,2,1:T(2,128)(2,1)S(1)} %get-tuple-element.11, bf16[4,20,20,2,80]{4,3,0,2,1:T(2,128)(2,1)S(1)} %get-tuple-element.12, bf16[4,20,20,2,80]{4,3,0,2,1:T(2,128)(2,1)S(1)} %get-tuple-element.9), kind=kLoop, calls=%fused_computation.36 | loop fusion | flops 8192000 | bytes 4096000 | tf_op jit(solution)/shard_map/transpose | solution.py:57
  102.2 4.1 %copy.47 = bf16[8,4,20,20,80]{4,3,2,1,0:T(8,128)(2,1)} copy(bf16[8,4,20,20,80]{4,0,1,2,3:T(8,128)(2,1)S(1)} %maximum_bitcast_fusion) | data formatting | bytes 4096000 | tf_op jit(solution)/shard_map/transpose | solution.py:57
  106.3 5.3 %reshape.385 = bf16[8,80,1600]{2,1,0:T(8,128)(2,1)S(1)} reshape(bf16[8,4,20,20,80]{4,3,2,1,0:T(8,128)(2,1)} %copy.47) | data formatting | bytes 4096000 | tf_op jit(solution)/shard_map/reshape | solution.py:58
  111.6 55.9 %all_to_all.20 = bf16[8,80,1600]{2,1,0:T(8,128)(2,1)} all-to-all(bf16[8,80,1600]{2,1,0:T(8,128)(2,1)S(1)} %reshape.385), channel_id=1, replica_groups=mesh['pair'=4,'fold'=8] {'fold'}, dimensions={0} | all-to-all | bytes 4096000 | tf_op jit(solution)/shard_map/all_to_all | solution.py:59
  169.2 56.1 %fusion.14 = bf16[80,80,2,160]{3,2,1,0:T(2,128)(2,1)} fusion(bf16[80,80,2,640]{3,2,1,0:T(2,128)(2,1)} %param.7, s32[160]{0:T(256)S(1)} %get-tuple-element.22, s32[80,80,2]{2,1,0:T(8,128)S(1)} %broadcast_xor_fusion, s32[160]{0:T(256)S(1)} %get-tuple-element.23, s32[160]{0:T(256)S(1)} %copy-done.2, s32[160]{0:T(256)S(1)} %get-tuple-element.21), kind=kLoop, calls=%fused_computation.22 | loop fusion | flops 22528000 | bytes 20533760 | tf_op jit(solution)/shard_map/add | solution.py:67
  225.3 15.1 %reshape.394 = bf16[80,4,20,320]{3,2,1,0:T(8,128)(2,1)} reshape(bf16[80,80,2,160]{3,2,1,0:T(2,128)(2,1)} %fusion.14) | data formatting | bytes 8192000 | tf_op jit(solution)/shard_map/reshape | solution.py:68
  240.4 6.7 %copy.64 = bf16[80,4,20,320]{3,0,2,1:T(8,128)(2,1)} copy(bf16[80,4,20,320]{3,2,1,0:T(8,128)(2,1)} %reshape.394) | data formatting | bytes 8192000 | tf_op jit(solution)/shard_map/reshape | solution.py:68
  247.7 4.3 %fusion.39 = (bf16[1,20,80,320]{3,2,1,0:T(8,128)(2,1)S(1)}, bf16[1,20,80,320]{3,2,1,0:T(8,128)(2,1)S(1)}, bf16[1,20,80,320]{3,2,1,0:T(8,128)(2,1)}, bf16[1,20,80,320]{3,2,1,0:T(8,128)(2,1)}) fusion(bf16[4,20,80,320]{3,2,1,0:T(8,128)(2,1)} %bitcast.46), kind=kLoop, calls=%fused_computation.94 | loop fusion | bytes 8192000 | tf_op jit(solution)/shard_map/slice | solution.py:78
  252.0 8.3 %fusion.1 = f32[320,4,8,80]{0,3,2,1:T(8,128)S(1)} fusion(bf16[1600,320,1,1]{1,0,3,2:T(8,128)(2,1)} %bitcast.55, bf16[4,8,80,1600]{3,2,1,0:T(8,128)(2,1)} %bitcast.58, s32[1600]{0:T(1024)S(1)} %xor.329, s32[4,8,80]{2,1,0:T(8,128)S(1)} %broadcast_xor_fusion.8), kind=kOutput, calls=%fused_computation.9 | convolution fusion | flops 2629632000 | bytes 12509440 | tf_op jit(solution)/shard_map/pfrx,xn->fprn/dot_general | solution.py:77
  260.3 7.1 %fusion = f32[320,4,8,80]{0,3,2,1:T(8,128)} fusion(bf16[1600,320,1,1]{1,0,3,2:T(8,128)(2,1)S(1)} %bitcast.54, bf16[4,8,80,1600]{3,2,1,0:T(8,128)(2,1)S(1)} %bitcast.59, s32[1600]{0:T(1024)S(1)} %xor.306, s32[4,8,80]{2,1,0:T(8,128)S(1)} %broadcast_xor_fusion.8), kind=kOutput, calls=%fused_computation.8 | convolution fusion | flops 2629632000 | bytes 12509440 | tf_op jit(solution)/shard_map/pfrx,xn->fprn/dot_general | solution.py:77
  267.4 7.1 %fusion.2 = f32[320,4,8,80]{0,3,2,1:T(8,128)} fusion(bf16[1600,320,1,1]{1,0,3,2:T(8,128)(2,1)S(1)} %bitcast.53, bf16[4,8,80,1600]{3,2,1,0:T(8,128)(2,1)S(1)} %bitcast.60, s32[1600]{0:T(1024)S(1)} %xor.332, s32[4,8,80]{2,1,0:T(8,128)S(1)} %broadcast_xor_fusion.8), kind=kOutput, calls=%fused_computation.10 | convolution fusion | flops 2629632000 | bytes 12509440 | tf_op jit(solution)/shard_map/pfrx,xn->fprn/dot_general | solution.py:77
  274.5 8.2 %add_bitcast_fusion = f32[8,4,80,320]{3,2,0,1:T(8,128)S(1)} fusion(f32[320,4,8,80]{0,3,2,1:T(8,128)} %fusion.2, f32[320,4,8,80]{0,3,2,1:T(8,128)} %fusion, f32[320,4,8,80]{0,3,2,1:T(8,128)S(1)} %fusion.1, bf16[1600,320,1,1]{1,0,3,2:T(8,128)(2,1)S(1)} %bitcast.52, bf16[4,8,80,1600]{3,2,1,0:T(8,128)(2,1)S(1)} %bitcast.61, s32[1600]{0:T(1024)S(1)} %xor.335, ...), kind=kOutput, calls=%fused_computation.32 | convolution fusion | flops 2632089600 | bytes 22339840 | tf_op jit(solution)/shard_map/pfrx,xn->fprn/dot_general | solution.py:77
  285.1 82.2 %reduce-scatter.2.cloned.1.call-done = f32[320,320]{1,0:T(8,128)} async-done(((f32[2560,320]{1,0:T(8,128)}), f32[320,320]{1,0:T(8,128)}) %reduce-scatter.2.cloned.1.call-update) | async-done | bytes 409616 | tf_op jit(solution)/shard_map/reduce_scatter | solution.py:81
  368.8 4.5 %compare_select_fusion.32 = bf16[4,80,2,640]{3,2,1,0:T(2,128)(2,1)} fusion(bf16[4,80,2,160]{3,2,1,0:T(2,128)(2,1)S(1)} %bitcast.50, s32[640]{0:T(1024)S(1)} %convert_reduce_fusion, s32[4,80,2]{2,1,0:T(8,128)S(1)} %broadcast_xor_fusion.1), kind=kLoop, calls=%fused_computation.53 | loop fusion | flops 4096000 | bytes 1029120 | tf_op jit(solution)/shard_map/jit(_where)/select_n | solution.py:86
  (75 shorter events, 16.2 us)
Async XLA Ops:
  7.5 22.6 %copy-start.1 = (s32[160]{0:T(256)}, s32[160]{0:T(256)S(1)}, u32[]{:S(2)}) copy-start(s32[160]{0:T(256)S(1)} %get-tuple-element.24) | copy-start | bytes 1924
  7.6 12.2 %copy-start.3 = (s32[80]{0:T(128)}, s32[80]{0:T(128)S(1)}, u32[]{:S(2)}) copy-start(s32[80]{0:T(128)S(1)} %dynamic_slice.15) | copy-start | bytes 964
  10.1 9.7 %copy-start.11 = (s32[4]{0:T(128)}, s32[4]{0:T(128)S(1)}, u32[]{:S(2)}) copy-start(s32[4]{0:T(128)S(1)} %select_reduce_fusion) | copy-start | bytes 52
  25.2 42.7 %all-to-all-start = ((bf16[4,20,4,20,160]{4,0,3,1,2:T(4,128)(2,1)}), bf16[4,20,4,20,160]{4,0,3,1,2:T(4,128)(2,1)S(1)}, u32[]{:S(2)}, u32[]{:S(2)}) async-start(bf16[4,20,4,20,160]{4,0,3,1,2:T(4,128)(2,1)} %copy.46), calls=%async_computation | async-start | bytes 6553600 | tf_op jit(solution)/shard_map/all_to_all | solution.py:43
  29.5 222.5 %all-gather.3.cloned.1.call-start = ((), (), s32[]{:S(2)}) async-start(), calls=%async_computation.4 | async-start | bytes 10649600 | tf_op jit(solution)/shard_map/all_gather | solution.py:60
  70.5 10.2 %copy-start.5 = (s32[20]{0:T(128)S(1)}, s32[20]{0:T(128)}, u32[]{:S(2)}) copy-start(s32[20]{0:T(128)} %get-tuple-element.29) | copy-start | bytes 244
  70.5 10.2 %copy-start.6 = (s32[20]{0:T(128)S(1)}, s32[20]{0:T(128)}, u32[]{:S(2)}) copy-start(s32[20]{0:T(128)} %get-tuple-element.30) | copy-start | bytes 244
  70.5 10.2 %copy-start.8 = (s32[20]{0:T(128)S(1)}, s32[20]{0:T(128)}, u32[]{:S(2)}) copy-start(s32[20]{0:T(128)} %get-tuple-element.31) | copy-start | bytes 244
  111.5 56.1 %copy-start.4 = (s32[80]{0:T(128)S(1)}, s32[80]{0:T(128)}, u32[]{:S(2)}) copy-start(s32[80]{0:T(128)} %copy-done.3) | copy-start | bytes 964
  111.5 56.1 %copy-start.7 = (s32[20]{0:T(128)S(1)}, s32[20]{0:T(128)}, u32[]{:S(2)}) copy-start(s32[20]{0:T(128)} %get-tuple-element.30) | copy-start | bytes 244
  111.6 56.1 %copy-start.9 = (s32[20]{0:T(128)S(1)}, s32[20]{0:T(128)}, u32[]{:S(2)}) copy-start(s32[20]{0:T(128)} %get-tuple-element.31) | copy-start | bytes 244
  111.6 56.1 %copy-start.10 = (s32[20]{0:T(128)S(1)}, s32[20]{0:T(128)}, u32[]{:S(2)}) copy-start(s32[20]{0:T(128)} %get-tuple-element.32) | copy-start | bytes 244
  111.6 56.3 %copy-start.14 = (s32[8]{0:T(128)S(1)}, s32[8]{0:T(128)}, u32[]{:S(2)}) copy-start(s32[8]{0:T(128)} %param.11) | copy-start | bytes 100
  111.6 57.6 %copy-start.2 = (s32[160]{0:T(256)S(1)}, s32[160]{0:T(256)}, u32[]{:S(2)}) copy-start(s32[160]{0:T(256)} %copy-done.1) | copy-start | bytes 1924
  167.5 199.8 %reduce-scatter.2.cloned.1.call-start = ((), (), s32[]{:S(2)}) async-start(), calls=%async_computation.3 | async-start | bytes 4423680 | tf_op jit(solution)/shard_map/reduce_scatter | solution.py:81
  240.4 6.7 %copy-start.12 = (s32[4]{0:T(128)S(1)}, s32[4]{0:T(128)}, u32[]{:S(2)}) copy-start(s32[4]{0:T(128)} %copy-done.11) | copy-start | bytes 52
  252.0 8.3 %copy-start = (bf16[1,20,80,320]{3,2,1,0:T(8,128)(2,1)S(1)}, bf16[1,20,80,320]{3,2,1,0:T(8,128)(2,1)}, u32[]{:S(2)}) copy-start(bf16[1,20,80,320]{3,2,1,0:T(8,128)(2,1)} %get-tuple-element.8) | copy-start | bytes 3072004
  252.0 8.3 %copy-start.13 = (bf16[32,80,1600]{2,1,0:T(8,128)(2,1)S(1)}, bf16[32,80,1600]{2,1,0:T(8,128)(2,1)}, u32[]{:S(2)}) copy-start(bf16[32,80,1600]{2,1,0:T(8,128)(2,1)} %all-gather.3.cloned.1.call-done) | copy-start | bytes 24576004
Sparse Core Ops, SparseCore 0:
  167.6 56.5 all-gather.2
  285.0 82.2 reduce-scatter.1

commit v2 on v1

v2 whole, which is shorter than its diff:
```python
import functools

import jax
import jax.numpy as jnp
from jax import lax
from jax.experimental import pallas as pl
from jax.experimental.pallas import tpu as pltpu
from jax.sharding import PartitionSpec as P

LANES = 128
EARLY = 2
FOLDS = 4


def irrep_labels(sizes, count):
    boundaries = jnp.cumsum(sizes)
    positions = jnp.arange(count, dtype=jnp.int32)
    return jnp.sum((positions[:, None] >= boundaries[None, :]).astype(jnp.int32), axis=1)


def label_lookup(orbitals, labels, count):
    matches = orbitals[:, None] == jnp.arange(count, dtype=jnp.int32)[None, :]
    return jnp.sum(jnp.where(matches, labels[None, :], 0), axis=1)


def multiply_kernel(lhs_ref, *refs):
    rhs_refs, (row_ref, col_ref, out_ref) = refs[:FOLDS], refs[FOLDS:]
    n_pair = lhs_ref.shape[0]
    j_local = rhs_refs[0].shape[0]
    rows = row_ref[0].astype(jnp.bfloat16)
    left = jnp.concatenate([lhs_ref[p, 0] for p in range(n_pair)], axis=0)
    totals = [None] * j_local
    for s in range(FOLDS):
        keep = rows == col_ref[s].astype(jnp.bfloat16)
        part = jnp.where(keep, left, jnp.zeros_like(left))
        for j in range(j_local):
            term = jnp.dot(part, rhs_refs[s][j], preferred_element_type=jnp.float32)
            totals[j] = term if s == 0 else totals[j] + term
    for j, total in enumerate(totals):
        count, width = total.shape
        rest = width - LANES
        step = count * rest // LANES
        base = j * (count + step)
        out_ref[0, base:base + count] = total[:, :LANES]
        out_ref[0, base + count:base + count + step] = jnp.concatenate(
            [total[t * step:(t + 1) * step, LANES:] for t in range(LANES // rest)], axis=1
        )


def multiply(gathered, packed_w, row_labels, col_labels):
    n_pair, n_fold, span, depth = gathered.shape
    j_local, _, width = packed_w[0].shape
    rows = n_pair * span
    lines = j_local * rows * width // LANES
    rhs_spec = pl.BlockSpec(packed_w[0].shape, lambda f: (0, 0, 0), pipeline_mode=pl.Buffered(1))
    return pl.pallas_call(
        multiply_kernel,
        grid=(n_fold,),
        out_shape=jax.ShapeDtypeStruct((n_fold, lines, LANES), jnp.float32),
        in_specs=[pl.BlockSpec((n_pair, 1, span, depth), lambda f: (0, f, 0, 0))]
        + [rhs_spec] * FOLDS
        + [
            pl.BlockSpec((1, rows, 1), lambda f: (f, 0, 0)),
            pl.BlockSpec(col_labels.shape, lambda f: (0, 0, 0)),
        ],
        out_specs=pl.BlockSpec((1, lines, LANES), lambda f: (f, 0, 0)),
        compiler_params=pltpu.CompilerParams(vmem_limit_bytes=48 << 20),
        cost_estimate=pl.CostEstimate(
            flops=2 * n_fold * rows * FOLDS * depth * j_local * width,
            bytes_accessed=2 * gathered.size + 2 * FOLDS * packed_w[0].size,
            transcendentals=0,
        ),
    )(gathered, *packed_w, row_labels, col_labels)


def refold_kernel(occ_ref, moved_ref, row_ref, vir_ref, out_ref, wide_ref):
    n_pair, n_i, k_local, a_sub, v_pack = moved_ref.shape
    here, _, depth = out_ref.shape
    c_local = v_pack // here
    k_pack = depth // c_local
    for i in range(n_i):
        labels = row_ref[i] ^ vir_ref[0]
        for kappa in range(k_pack):
            total = jnp.zeros((a_sub, v_pack), jnp.float32)
            for s in range(FOLDS):
                k = s * k_pack + kappa
                piece = moved_ref[k // k_local, i, k % k_local].astype(jnp.float32)
                total = jnp.where(labels == occ_ref[k], piece, total)
            for f in range(here):
                wide_ref[f, i * a_sub:(i + 1) * a_sub, kappa * c_local:(kappa + 1) * c_local] = (
                    total[:, f * c_local:(f + 1) * c_local]
                )
    out_ref[...] = wide_ref[...].astype(out_ref.dtype)


def refold(moved, row_labels, vir_labels, occ_labels, c_local):
    _, n_i, _, a_sub, v_pack = moved.shape
    here = v_pack // c_local
    shape = (FOLDS * here, n_i * a_sub, occ_labels.shape[0] // FOLDS * c_local)
    return pl.pallas_call(
        refold_kernel,
        grid=(FOLDS,),
        out_shape=jax.ShapeDtypeStruct(shape, moved.dtype),
        in_specs=[
            pl.BlockSpec(memory_space=pltpu.SMEM),
            pl.BlockSpec(moved.shape, lambda q: (0, 0, 0, 0, 0), pipeline_mode=pl.Buffered(1)),
            pl.BlockSpec((n_i, a_sub, 1), lambda q: (0, 0, 0)),
            pl.BlockSpec((1, 1, v_pack), lambda q: (q, 0, 0)),
        ],
        out_specs=pl.BlockSpec((here,) + shape[1:], lambda q: (q, 0, 0)),
        scratch_shapes=[pltpu.VMEM((here,) + shape[1:], jnp.float32)],
        compiler_params=pltpu.CompilerParams(vmem_limit_bytes=40 << 20),
    )(occ_labels, moved, row_labels[..., None], vir_labels.reshape(FOLDS, 1, v_pack))


def body(n_pair, n_fold, amplitudes, cycle_block, occ_sizes, vir_sizes, window_i, window_occ):
    c_local, occ_total, j_local, vir_total = cycle_block.shape
    n_i, k_local, a_rows, _ = amplitudes.shape
    v_pack = vir_total // FOLDS
    k_pack = occ_total // FOLDS
    a_sub = a_rows // n_pair
    fold = lax.axis_index("fold")
    pair = lax.axis_index("pair")
    occ_labels = irrep_labels(occ_sizes, occ_total)
    vir_labels = irrep_labels(vir_sizes, vir_total)
    c_labels = lax.dynamic_slice_in_dim(vir_labels, fold * c_local, c_local)
    a_labels = lax.dynamic_slice_in_dim(vir_labels, fold * a_rows, a_rows)
    k_labels = lax.dynamic_slice_in_dim(occ_labels, pair * k_local, k_local)
    i_labels = label_lookup(window_i, occ_labels, occ_total)
    j_orbitals = lax.dynamic_slice_in_dim(window_occ, pair * j_local, j_local)
    j_labels = label_lookup(j_orbitals, occ_labels, occ_total)

    ika = i_labels[:, None, None] ^ k_labels[None, :, None] ^ a_labels[None, None, :]
    packed_c = 0
    for q in range(FOLDS):
        cut = slice(q * v_pack, (q + 1) * v_pack)
        keep = ika[..., None] == vir_labels[cut]
        packed_c = packed_c + jnp.where(keep, amplitudes[..., cut], 0)
    parts = packed_c.reshape(n_i, k_local, n_pair, a_sub, v_pack).transpose(2, 0, 1, 3, 4)
    moved = lax.all_to_all(parts, "pair", split_axis=0, concat_axis=0, tiled=True)
    depth = k_pack * c_local
    def pack_slices(source, wanted):
        made = []
        for s in wanted:
            block = source[:, s * k_pack:(s + 1) * k_pack].transpose(2, 1, 0, 3)
            own_k = occ_labels[s * k_pack:(s + 1) * k_pack]
            jkc = j_labels[:, None, None] ^ own_k[None, :, None] ^ c_labels[None, None, :]
            folded = 0
            for q in range(FOLDS):
                cut = slice(q * v_pack, (q + 1) * v_pack)
                keep = jkc[..., None] == vir_labels[cut]
                folded = folded + jnp.where(keep, block[..., cut], 0)
            made.append(folded.reshape(j_local, depth, v_pack))
        return made

    early = pack_slices(cycle_block, range(EARLY))
    moved, *early = lax.optimization_barrier((moved, *early))
    own_a = lax.dynamic_slice_in_dim(a_labels, pair * a_sub, a_sub)
    packed_k = refold(moved, i_labels[:, None] ^ own_a[None, :], vir_labels, occ_labels, c_local)
    packed_k, source = lax.optimization_barrier((packed_k, cycle_block))
    packed_w = list(early) + pack_slices(source, range(EARLY, FOLDS))
    relaid = lax.all_to_all(packed_k, "fold", split_axis=0, concat_axis=0, tiled=True)
    gathered = lax.all_gather(relaid, "pair", axis=0, tiled=False)

    row_a = vir_labels.reshape(n_fold, n_pair, a_sub)
    row_labels = (row_a[:, :, None, :] ^ i_labels[:, None]).reshape(n_fold, -1, 1)
    col_labels = (occ_labels[:, None] ^ c_labels[None, :]).reshape(FOLDS, 1, depth)
    count = n_pair * n_i * a_sub
    rest = v_pack - LANES
    step = count * rest // LANES
    partial_sum = multiply(gathered, packed_w, row_labels, col_labels)
    summed = lax.psum_scatter(
        partial_sum.reshape(-1, LANES), "fold", scatter_dimension=0, tiled=True
    ).astype(jnp.bfloat16)
    columns = []
    for j in range(j_local):
        own = summed[j * (count + step):(j + 1) * (count + step)]
        tail = jnp.concatenate(
            [own[count:, t * rest:(t + 1) * rest] for t in range(LANES // rest)], axis=0
        )
        columns.append(jnp.concatenate([own[:count], tail], axis=1))
    own = jnp.stack(columns, axis=1).reshape(n_pair, n_i, a_sub, j_local, v_pack)
    own = own.transpose(1, 0, 2, 3, 4).reshape(n_i, a_rows, j_local, v_pack)
    iaj = i_labels[:, None, None] ^ a_labels[None, :, None] ^ j_labels[None, None, :]
    keep = iaj[..., None] == vir_labels
    return jnp.where(keep, jnp.concatenate([own] * FOLDS, axis=-1), 0)


def solution(mesh):
    sizes = mesh.shape["pair"], mesh.shape["fold"]
    placed = (P(None, "pair", "fold", None), P("fold", None, "pair", None), P(), P(), P(), P())

    def run(*args):
        return body(*sizes, *args)

    return jax.shard_map(
        run, mesh=mesh, in_specs=placed, out_specs=P(None, "fold", "pair", None), check_vma=False
    )
```

time: 387 us -> 309 us (0.80); the launches traced: 380 us -> 309 us
  matrix products: 30.7 us -> 0 us
  Pallas kernels: 0 us -> 30.7 us
  local copies, waits for them, and re-layouts: 60.5 us -> 33.4 us
  waiting for transfers between devices: 117 us -> 90.5 us
  other arithmetic: 98.4 us -> 77.9 us
    reduce_scatter x1 -> x0, waiting for transfers between devices: 82.2 us -> none  [body(): own = lax.psum_scatter(flat, 'fold', scatter_dimension=0, tiled=True)]
    unnamed x2 -> x3, waiting for transfers between devices: 0.03 us -> 76.3 us
    all_to_all x1, waiting for transfers between devices: 34.4 us -> 0.01 us  [body(): lax.all_to_all(parts, 'pair', split_axis=0, concat_axis=0, tiled=True)]
    pallas_call x0 -> x2, Pallas kernels: none -> 30.7 us  [the longest x1 24.5 us: multiply(): pl.pallas_call(multiply_kernel, grid=(n_fold,), out_shape=jax.ShapeDtypeS...]
    dot_general x4 -> x0, matrix products: 30.7 us -> none  [body(): jnp.einsum('pfrx,xn->fprn', lhs, packed_w[s], preferred_element_type=jnp....]
    reshape x6 -> x1, local copies, waits for them, and re-layouts: 30.3 us -> 0.08 us  [refold(): vir_labels.reshape(FOLDS, 1, v_pack)]
    add x2, other arithmetic: 72.7 us -> 56.1 us  [pack_slices(): folded = folded + jnp.where(keep, block[..., cut], 0)]
    all_gather x1, waiting for transfers between devices: 0.01 us -> 14.2 us  [body(): gathered = lax.all_gather(relaid, 'pair', axis=0, tiled=False)]
  transfers between devices with their start and end apart: 3 -> 3, of which waited for: 2 -> 2; matrix products, arithmetic and copies ran while one was open for 23% -> 26% of each run, Pallas kernels for 0% -> 0%
where the time goes in v2:
time: 309 us
  waiting for transfers between devices  90.5 us (29%)
  other arithmetic  77.9 us (25%)
  blocking collectives  57.4 us (19%)
  local copies, waits for them, and re-layouts  33.4 us (11%)
  Pallas kernels  30.7 us (10%)
  between operations  13.7 us (4%)
  starting transfers between devices  5.08 us (2%)
    unnamed x3, waiting for transfers between devices  76.3 us
    all_to_all x1, blocking collectives, body(): lax.all_to_all(packed_k, 'fold', split_axis=0, concat_axis=0, tiled=True)  57.4 us
    add x2, other arithmetic, pack_slices(): folded = folded + jnp.where(keep, block[..., cut], 0)  56.1 us
    pallas_call x1, Pallas kernels, multiply(): pl.pallas_call(multiply_kernel, grid=(n_fold,), out_shape=jax.ShapeDtypeS...  24.5 us
    transpose x2, local copies, waits for them, and re-layouts, pack_slices(): block = source[:, s * k_pack:(s + 1) * k_pack].transpose(2, 1, 0, 3)  14.5 us
    all_gather x1, waiting for transfers between devices, body(): gathered = lax.all_gather(relaid, 'pair', axis=0, tiled=False)  14.2 us
    add x1, other arithmetic, body(): packed_c = packed_c + jnp.where(keep, amplitudes[..., cut], 0)  9.53 us
    pallas_call x1, Pallas kernels, refold(): pl.pallas_call(refold_kernel, grid=(FOLDS,), out_shape=jax.ShapeDtypeStru...  6.19 us
  transfers between devices with their start and end apart: 3, of which 2 were waited for; matrix products, arithmetic and copies ran while one was open for 26% of the time, Pallas kernels for 0%

profile of v2, /device:TPU:0, one launch (start us, length us, event | category | flops | bytes accessed | tf_op | source)
XLA Modules:
  0.0 308.5 jit_solution(14205314819769236511)
XLA Ops:
  8.6 0.8 select_reduce_fusion
  9.6 9.5 %fusion.2 = bf16[4,20,80,160]{3,2,1,0:T(8,128)(2,1)S(1)} fusion(bf16[4,20,80,640]{3,2,1,0:T(8,128)(2,1)} %param.6, s32[160]{0:T(256)S(1)} %get-tuple-element.34, s32[160]{0:T(256)S(1)} %get-tuple-element.35, s32[160]{0:T(256)S(1)} %get-tuple-element.36, s32[160]{0:T(256)S(1)} %get-tuple-element.33, s32[4,20,80]{2,1,0:T(8,128)S(1)} %broadcast_xor_fusion.7), kind=kLoop, calls=%fused_computation.26 | loop fusion | flops 11264000 | bytes 10268160 | tf_op jit(solution)/shard_map/add | solution.py:138
  19.1 2.5 copy.69
  21.7 2.9 copy.70
  24.6 4.8 %all-to-all-start = ((bf16[4,4,20,20,160]{4,1,3,2,0:T(4,128)(2,1)}), bf16[4,4,20,20,160]{4,1,3,2,0:T(4,128)(2,1)}, u32[]{:S(2)}, u32[]{:S(2)}) async-start(bf16[4,4,20,20,160]{4,1,3,2,0:T(4,128)(2,1)} %copy.70), calls=%async_computation | async-start | bytes 6553600 | tf_op jit(solution)/shard_map/all_to_all | solution.py:140
  29.7 7.1 %slice_bitcast_fusion.2 = (bf16[2,20,80,640]{3,0,1,2:T(2,128)(2,1)S(1)}, bf16[2,20,80,640]{3,0,1,2:T(2,128)(2,1)S(1)}) fusion(bf16[80,80,2,640]{3,2,1,0:T(2,128)(2,1)} %param.7), kind=kLoop, calls=%fused_computation.22 | loop fusion | bytes 16384000 | tf_op jit(solution)/shard_map/transpose | solution.py:145
  36.9 1.6 broadcast_xor_fusion.1
  38.6 28.3 %fusion.8 = (bf16[2,20,80,160]{3,0,1,2:T(2,128)(2,1)S(1)}, bf16[2,20,80,160]{3,0,1,2:T(2,128)(2,1)}) fusion(bf16[2,20,80,640]{3,0,1,2:T(2,128)(2,1)S(1)} %get-tuple-element.17, s32[2,20,80]{0,1,2:T(8,128)S(1)} %get-tuple-element.38, s32[160]{0:T(256)S(1)} %get-tuple-element.34, s32[160]{0:T(256)S(1)} %get-tuple-element.35, s32[160]{0:T(256)S(1)} %get-tuple-element.36, ...), kind=kLoop, calls=%fused_computation.33 | loop fusion | flops 11264000 | bytes 10268160 | tf_op jit(solution)/shard_map/add | solution.py:152
  67.3 1.1 copy-done.1
  68.9 2.6 copy.73.moved_ref
  71.5 6.2 %shard_map.64 = bf16[8,80,1600]{2,1,0:T(8,128)(2,1)S(1)} custom-call(s32[80]{0:T(128)S(1)} %convert_reduce_fusion.1.occ_ref, bf16[4,4,20,20,160]{4,3,2,1,0:T(8,128)(2,1)S(1)} %copy.73.moved_ref, s32[4,20,1]{2,1,0:T(8,128)S(1)} %broadcast_xor_fusion.6.row_ref, s32[4,1,160]{2,1,0:T(1,128)S(1)} %reshape.401.vir_ref), custom_call_target="tpu_custom_call" | custom-call | tf_op jit(solution)/shard_map/pallas_call | solution.py:100
  77.7 57.4 %all_to_all.10 = bf16[8,80,1600]{2,1,0:T(8,128)(2,1)} all-to-all(bf16[8,80,1600]{2,1,0:T(8,128)(2,1)S(1)} %shard_map.64), channel_id=1, replica_groups=mesh['pair'=4,'fold'=8] {'fold'}, dimensions={0} | all-to-all | bytes 4096000 | tf_op jit(solution)/shard_map/all_to_all | solution.py:162
  136.0 1.5 xor.321
  137.6 2.6 broadcast_xor_fusion.refs_4_
  140.2 7.5 %slice_bitcast_fusion = (bf16[2,20,80,640]{3,0,1,2:T(2,128)(2,1)S(1)}, bf16[2,20,80,640]{3,0,1,2:T(2,128)(2,1)S(1)}) fusion(bf16[80,80,2,640]{3,2,1,0:T(2,128)(2,1)} %param.7), kind=kLoop, calls=%fused_computation.20 | loop fusion | bytes 16384000 | tf_op jit(solution)/shard_map/transpose | solution.py:145
  147.7 27.8 %fusion.14 = (bf16[2,20,80,160]{3,0,1,2:T(2,128)(2,1)S(1)}, bf16[2,20,80,160]{3,0,1,2:T(2,128)(2,1)S(1)}) fusion(bf16[2,20,80,640]{3,0,1,2:T(2,128)(2,1)S(1)} %get-tuple-element.15, s32[2,20,80]{0,1,2:T(8,128)S(1)} %copy-done.2, s32[160]{0:T(256)S(1)} %get-tuple-element.34, s32[160]{0:T(256)S(1)} %get-tuple-element.35, s32[160]{0:T(256)S(1)} %get-tuple-element.36, ...), kind=kLoop, calls=%fused_computation.39 | loop fusion | flops 11264000 | bytes 10268160 | tf_op jit(solution)/shard_map/add | solution.py:152
  175.5 1.6 copy.74
  177.1 1.5 copy.75
  178.5 14.2 %all-gather.3.cloned.1.call-done = bf16[32,80,1600]{2,1,0:T(8,128)(2,1)} async-done(((bf16[8,80,1600]{2,1,0:T(8,128)(2,1)}), bf16[32,80,1600]{2,1,0:T(8,128)(2,1)}) %all-gather.3.cloned.1.call-update) | async-done | bytes 8192016 | tf_op jit(solution)/shard_map/all_gather | solution.py:163
  192.8 1.3 copy-done
  194.1 24.5 %shard_map.65 = f32[8,800,128]{2,1,0:T(8,128)} custom-call(bf16[4,8,80,1600]{3,2,1,0:T(8,128)(2,1)} %bitcast.33, bf16[2,1600,160]{2,1,0:T(8,128)(2,1)S(1)} %bitcast.26, bf16[2,1600,160]{2,1,0:T(8,128)(2,1)S(1)} %bitcast.25, bf16[2,1600,160]{2,1,0:T(8,128)(2,1)} %bitcast.29, bf16[2,1600,160]{2,1,0:T(8,128)(2,1)} %bitcast.30, s32[8,320,1]{2,1,0:T(8,128)S(1)} %copy-done, ...), custom_call_target="tpu_custom_call" | custom-call | flops 10485760000 | bytes 12288000 | tf_op jit(solution)/shard_map/pallas_call | solution.py:56
  218.7 76.2 %reduce-scatter.4.cloned.1.call-done = f32[800,128]{1,0:T(8,128)} async-done(((f32[6400,128]{1,0:T(8,128)}), f32[800,128]{1,0:T(8,128)}) %reduce-scatter.4.cloned.1.call-update) | async-done | bytes 409616
  295.0 1.2 copy.85
  297.2 4.5 %compare_select_fusion.20 = bf16[4,80,2,640]{3,2,1,0:T(2,128)(2,1)} fusion(bf16[4,80,2,160]{3,2,1,0:T(2,128)(2,1)S(1)} %bitcast.31, s32[640]{0:T(1024)S(1)} %convert_reduce_fusion, s32[4,80,2]{2,1,0:T(8,128)S(1)} %broadcast_xor_fusion.5), kind=kLoop, calls=%fused_computation.27 | loop fusion | flops 4096000 | bytes 1029120 | tf_op jit(solution)/shard_map/jit(_where)/select_n | solution.py:186
  (51 shorter events, 5.7 us)
Async XLA Ops:
  24.6 4.9 %copy-start.4 = (s32[8]{0:T(128)S(1)}, s32[8]{0:T(128)}, u32[]{:S(2)}) copy-start(s32[8]{0:T(128)} %param.11) | copy-start | bytes 100
  24.6 44.3 %all-to-all-start = ((bf16[4,4,20,20,160]{4,1,3,2,0:T(4,128)(2,1)}), bf16[4,4,20,20,160]{4,1,3,2,0:T(4,128)(2,1)}, u32[]{:S(2)}, u32[]{:S(2)}) async-start(bf16[4,4,20,20,160]{4,1,3,2,0:T(4,128)(2,1)} %copy.70), calls=%async_computation | async-start | bytes 6553600 | tf_op jit(solution)/shard_map/all_to_all | solution.py:140
  29.4 163.3 %all-gather.3.cloned.1.call-start = ((), (), s32[]{:S(2)}) async-start(), calls=%async_computation.3 | async-start | bytes 10649600 | tf_op jit(solution)/shard_map/all_gather | solution.py:163
  67.0 1.4 copy-start.1
  135.2 159.8 %reduce-scatter.4.cloned.1.call-start = ((), (), s32[]{:S(2)}) async-start(), calls=%async_computation.4 | async-start | bytes 3686400
  140.2 7.5 %copy-start.2 = (s32[2,20,80]{0,1,2:T(8,128)S(1)}, s32[2,20,80]{0,1,2:T(8,128)}, u32[]{:S(2)}) copy-start(s32[2,20,80]{0,1,2:T(8,128)} %get-tuple-element.37) | copy-start | bytes 38404
  140.2 7.5 %copy-start.3 = (s32[2,20,80]{0,1,2:T(8,128)S(1)}, s32[2,20,80]{0,1,2:T(8,128)}, u32[]{:S(2)}) copy-start(s32[2,20,80]{0,1,2:T(8,128)} %get-tuple-element.39) | copy-start | bytes 38404
  192.8 1.3 copy-start
Sparse Core Ops, SparseCore 0:
  135.3 57.4 all-gather.2
  218.7 76.2 reduce-scatter.3
